TPU v7x, 32 devices: a whole 2x2x4 slice. The times are simulated.
32 devices in a mesh: parts: 2 (over y), expert: 4 (over z), tensor: 4 (over x, core).
Axes of the slice: x: 2, y: 2, z: 4, core: 2. Of those that a mesh axis runs over, the one named last changes fastest.
Arguments:
- mamba_input: bfloat16 [128, 4096], P(('parts', 'expert'), 'tensor'), parts along dimension 0, may hold values from -5 to 5
- mamba_gate: bfloat16 [128, 4096], P(('parts', 'expert'), 'tensor'), parts along dimension 0, may hold values from -5 to 5
- conv_state: bfloat16 [128, 3, 4096], P(('parts', 'expert'), None, 'tensor'), parts along dimension 0, may hold values from -5 to 5
- scan_state: float32 [128, 16, 4096], P(('parts', 'expert'), None, 'tensor'), parts along dimension 0, may hold values from -6 to 6
- conv_weight: float32 [4, 4096], P(None, 'tensor'), may hold values from -3 to 3
- conv_bias: float32 [4096], P('tensor'), may hold values from -0.5 to 0.5
- state_proj: bfloat16 [288, 4096], P(None, 'tensor'), may hold values from -0.09375 to 0.09375
- step_proj: bfloat16 [256, 4096], P(None, 'tensor'), may hold values from -0.375 to 0.375
- step_bias: float32 [4096], P('tensor'), may hold values from -4.5 to -1
- decay_log: float32 [16, 4096], P(None, 'tensor'), may hold values from 0 to 2.8
- skip_gain: float32 [4096], P('tensor'), may hold values from 0.5 to 2
- queries: bfloat16 [128, 32, 128], P(('parts', 'expert'), 'tensor'), parts along dimension 0, may hold values from -48 to 48
- new_entry: bfloat16 [128, 8, 256], P(('parts', 'expert'), 'tensor'), parts along dimension 0, may hold values from -4 to 4
- past_entries: bfloat16 [128, 8, 128, 256], P(('parts', 'expert'), 'tensor'), parts along dimension 0, may hold values from -4 to 4
- lengths: int32 [128], P(('parts', 'expert')), parts along dimension 0, may hold values from 2 to 128, as said below
- expert_input: bfloat16 [128, 2048], P(('parts', 'expert'), 'tensor'), parts along dimension 0, may hold values from -5 to 5
- routes: int32 [128, 2], P(('parts', 'expert')), parts along dimension 0, may hold values from 0 to 7, as said below
- slots: int32 [128, 2], P(('parts', 'expert')), parts along dimension 0, may hold values from 0 to 7, as said below
- gates: float32 [128, 2], P(('parts', 'expert')), parts along dimension 0, may hold values from 0.1 to 1
- inner_weights: bfloat16 [8, 2, 8192, 2048], P('expert', None, 'tensor'), may hold values from -0.125 to 0.125
- outer_weights: bfloat16 [8, 8192, 2048], P('expert', 'tensor'), may hold values from -0.09375 to 0.09375
Outputs:
- mamba_out: bfloat16 [128, 4096], P(('parts', 'expert'), 'tensor'), parts along dimension 0
- next_state: float32 [128, 16, 4096], P(('parts', 'expert'), None, 'tensor'), parts along dimension 0
- attention_out: bfloat16 [128, 4096], P(('parts', 'expert'), 'tensor'), parts along dimension 0
- expert_out: bfloat16 [128, 2048], P(('parts', 'expert'), 'tensor'), parts along dimension 0
There are 2 independent parts, one for each index of `parts`. A program takes and returns all parts, laid end to end along the dimension named above; an argument that names none is the same for every part. Nothing has to cross between parts.
Inputs may be any that keep to these rules, and one draw needn't show every extreme that they name: `routes`: A row names 2 different experts. Within the 16 rows of one device (aligned blocks) no expert is named more than 8 times, and one expert, the same in all blocks, is named exactly 8 times in every block. slots[t, k] numbers the rows of t's block that name expert routes[t, k]: within a block the slots of one expert are distinct. `lengths`: every block of 16 sequences holds one of length 128.
All inputs are finite; a program needn't handle non-finite values.
Results may differ from a plain program's by a relative error of at most 0.006.
Values may be sent and summed in bfloat16 or wider, within the bound.
A program may use at most 128 MiB of HBM per device.

v0:
```python
import jax
import jax.numpy as jnp
from jax import lax
from jax.sharding import PartitionSpec as P

EXPERTS = 8


def mamba_step(
    mamba_input,
    mamba_gate,
    conv_state,
    scan_state,
    conv_weight,
    conv_bias,
    state_proj,
    step_proj,
    step_bias,
    decay_log,
    skip_gain,
):
    window = jnp.concatenate(
        [conv_state.astype(jnp.float32), mamba_input.astype(jnp.float32)[:, None, :]], axis=1
    )
    conv_act = jax.nn.silu(jnp.sum(window * conv_weight[None], axis=1) + conv_bias)
    local_mix = lax.dot_general(
        conv_act.astype(jnp.bfloat16),
        state_proj,
        (((1,), (1,)), ((), ())),
        preferred_element_type=jnp.float32,
    )
    mixing = lax.psum(local_mix, "tensor")
    low_rank = step_proj.shape[0]
    states = decay_log.shape[0]
    step_size = jax.nn.softplus(
        jnp.dot(
            mixing[:, :low_rank].astype(jnp.bfloat16), step_proj, preferred_element_type=jnp.float32
        )
        + step_bias
    )
    in_coef = mixing[:, low_rank : low_rank + states]
    out_coef = mixing[:, low_rank + states :]
    decay_rate = jnp.exp(-step_size[:, None, :] * jnp.exp(decay_log)[None])
    next_state = decay_rate * scan_state + (step_size * conv_act)[:, None, :] * in_coef[:, :, None]
    mixed_out = jnp.sum(next_state * out_coef[:, :, None], axis=1) + skip_gain * conv_act
    return (
        (mixed_out * jax.nn.silu(mamba_gate.astype(jnp.float32))).astype(jnp.bfloat16),
        next_state,
    )


def attend(queries, new_entry, past_entries, lengths):
    seq_count, head_count, head_size = queries.shape
    groups = past_entries.shape[1]
    per_group = head_count // groups
    positions = past_entries.shape[2]
    scaling = head_size ** (-0.5)
    query_rows = queries.reshape(seq_count, groups, per_group, head_size)
    scores = (
        jnp.einsum(
            "sgqd,sgld->sgql",
            query_rows,
            past_entries[..., :head_size],
            preferred_element_type=jnp.float32,
        )
        * scaling
    )
    own_score = (
        jnp.einsum(
            "sgqd,sgd->sgq",
            query_rows,
            new_entry[..., :head_size],
            preferred_element_type=jnp.float32,
        )
        * scaling
    )
    live_mask = jnp.arange(positions, dtype=jnp.int32)[None, :] < lengths[:, None]
    scores = jnp.where(live_mask[:, None, None, :], scores, -jnp.inf)
    highest = jnp.maximum(jnp.max(scores, axis=3), own_score)
    weights = jnp.exp(scores - highest[..., None])
    own_weight = jnp.exp(own_score - highest)
    denominator = jnp.sum(weights, axis=3) + own_weight
    weights_low = (weights / denominator[..., None]).astype(jnp.bfloat16)
    own_low = (own_weight / denominator).astype(jnp.bfloat16)
    mixed_out = jnp.einsum(
        "sgql,sgld->sgqd",
        weights_low,
        past_entries[..., head_size:],
        preferred_element_type=jnp.float32,
    )
    mixed_out = (
        mixed_out
        + own_low.astype(jnp.float32)[..., None]
        * new_entry[..., head_size:].astype(jnp.float32)[:, :, None, :]
    )
    return mixed_out.reshape(seq_count, head_count * head_size).astype(jnp.bfloat16)


def shards(
    mamba_input,
    mamba_gate,
    conv_state,
    scan_state,
    conv_weight,
    conv_bias,
    state_proj,
    step_proj,
    step_bias,
    decay_log,
    skip_gain,
    queries,
    new_entry,
    past_entries,
    lengths,
    expert_input,
    routes,
    slots,
    gates,
    inner_weights,
    outer_weights,
):
    peer_count = lax.axis_size("expert")
    token_count = routes.shape[0]
    capacity = max(2, 4 * token_count // EXPERTS)
    replicas = max(1, peer_count // EXPERTS)
    local_rows = inner_weights.shape[0]
    total_rows = peer_count * local_rows
    row_expert = jnp.arange(total_rows, dtype=jnp.int32) // replicas
    slot_index = jnp.arange(capacity, dtype=jnp.int32)
    matches = (row_expert[:, None, None, None] == routes[None, None, :, :]) & (
        slot_index[None, :, None, None] == slots[None, None, :, :]
    )
    send_table = jnp.any(matches, axis=3).astype(jnp.bfloat16)
    weight_table = jnp.sum(jnp.where(matches, gates[None, None, :, :], 0.0), axis=3)
    features = lax.all_gather(expert_input, "tensor", axis=1, tiled=True)
    outgoing = jnp.einsum(
        "rcb,bd->rcd", send_table, features, preferred_element_type=jnp.float32
    ).astype(jnp.bfloat16)
    outgoing = outgoing.reshape(peer_count, local_rows, capacity, features.shape[1])
    gate_rows = inner_weights[:, 0]
    up_rows = inner_weights[:, 1]
    received = lax.all_to_all(outgoing, "expert", split_axis=0, concat_axis=0, tiled=True)
    gate_val = jnp.einsum("nlcd,lfd->nlcf", received, gate_rows, preferred_element_type=jnp.float32)
    up_val = jnp.einsum("nlcd,lfd->nlcf", received, up_rows, preferred_element_type=jnp.float32)
    hidden = (jax.nn.silu(gate_val) * up_val).astype(jnp.bfloat16)
    partial_value = jnp.einsum(
        "nlcf,lfd->nlcd", hidden, outer_weights, preferred_element_type=jnp.float32
    )
    share_sum = lax.psum_scatter(partial_value, "tensor", scatter_dimension=3, tiled=True)
    returned = lax.all_to_all(share_sum, "expert", split_axis=0, concat_axis=0, tiled=True)
    returned = returned.reshape(total_rows, capacity, returned.shape[3])
    merged = jnp.einsum("rcb,rcd->bd", weight_table, returned, precision=lax.Precision.HIGHEST)
    expert_out = merged.astype(jnp.bfloat16)
    mamba_out, next_state = mamba_step(
        mamba_input,
        mamba_gate,
        conv_state,
        scan_state,
        conv_weight,
        conv_bias,
        state_proj,
        step_proj,
        step_bias,
        decay_log,
        skip_gain,
    )
    attention_out = attend(queries, new_entry, past_entries, lengths)
    return (mamba_out, next_state, attention_out, expert_out)


def solution(mesh):
    return jax.shard_map(
        shards,
        mesh=mesh,
        in_specs=(
            P(("parts", "expert"), "tensor"),
            P(("parts", "expert"), "tensor"),
            P(("parts", "expert"), None, "tensor"),
            P(("parts", "expert"), None, "tensor"),
            P(None, "tensor"),
            P("tensor"),
            P(None, "tensor"),
            P(None, "tensor"),
            P("tensor"),
            P(None, "tensor"),
            P("tensor"),
            P(("parts", "expert"), "tensor", None),
            P(("parts", "expert"), "tensor", None),
            P(("parts", "expert"), "tensor", None, None),
            P(("parts", "expert")),
            P(("parts", "expert"), "tensor"),
            P(("parts", "expert"), None),
            P(("parts", "expert"), None),
            P(("parts", "expert"), None),
            P("expert", None, "tensor", None),
            P("expert", "tensor", None),
        ),
        out_specs=(
            P(("parts", "expert"), "tensor"),
            P(("parts", "expert"), None, "tensor"),
            P(("parts", "expert"), "tensor"),
            P(("parts", "expert"), "tensor"),
        ),
        check_vma=False,
    )
```

profile of v0, /device:TPU:0, one launch (start us, length us, event | category | flops | bytes accessed | tf_op | source)
XLA Modules:
  0.0 100.1 jit_solution(2538967461487775858)
XLA Ops:
  7.2 0.7 iota_compare_fusion
  7.9 0.7 iota_compare_fusion.1
  8.6 6.4 %all_gather.3 = bf16[16,2048]{1,0:T(8,128)(2,1)S(1)} all-gather(bf16[16,512]{1,0:T(8,128)(2,1)} %param.36), channel_id=1, replica_groups=mesh['parts'=2,'expert'=4,'tensor'=4] {'tensor'}, dimensions={1}, use_global_device_ids=true | all-gather | bytes 81920 | tf_op jit(solution)/shard_map/all_gather | solution.py:135
  15.1 0.9 convolution_convert_fusion
  16.0 5.3 %all-to-all-start = ((bf16[4,2,8,2048]{3,2,1,0:T(8,128)(2,1)}), bf16[4,2,8,2048]{3,2,1,0:T(8,128)(2,1)S(1)}, u32[]{:S(2)}, u32[]{:S(2)}) async-start(bf16[4,2,8,2048]{3,2,1,0:T(8,128)(2,1)} %bitcast.6), calls=%async_computation | async-start | bytes 524288 | tf_op jit(solution)/shard_map/all_to_all | solution.py:142
  21.3 0.7 iota_compare_fusion.2
  22.0 0.7 slice_bitcast_fusion
  22.8 0.9 fusion.42
  23.7 2.0 %fusion.49 = (f32[16,2,4]{2,1,0:T(2,128)S(1)}, f32[16,2,4,128]{3,2,1,0:T(4,128)S(1)}) fusion(bf16[16,2,4,128]{3,2,1,0:T(4,128)(2,1)} %bitcast.69, bf16[16,2,128,256]{3,2,1,0:T(8,128)(2,1)} %param.34, pred[16,128]{1,0:T(8,128)(4,1)S(1)} %iota_compare_fusion.2), kind=kOutput, calls=%fused_computation.64 | convolution fusion | flops 4243328 | bytes 1149440 | tf_op jit(solution)/shard_map/sgqd,sgld->sgql/dot_general | solution.py:60
  26.0 0.9 exp.29
  26.8 1.7 %fusion.24 = bf16[16,2,4,128]{3,2,1,0:T(4,128)(2,1)S(1)} fusion(bf16[16,2,128,256]{3,2,1,0:T(8,128)(2,1)} %param.34, f32[16,2,4,128]{3,2,1,0:T(4,128)S(1)} %get-tuple-element.15, f32[16,2,128]{2,1,0:T(2,128)S(1)} %get-tuple-element.13, f32[16,2,4]{2,1,0:T(2,128)S(1)} %get-tuple-element.9, f32[16,2,4]{2,1,0:T(2,128)S(1)} %get-tuple-element.8, ...), kind=kOutput, calls=%fused_computation.18 | convolution fusion | flops 4292608 | bytes 1164800 | tf_op jit(solution)/shard_map/sgql,sgld->sgqd/dot_general | solution.py:85
  28.5 0.6 convert_element_type.48
  29.1 0.9 multiply_reduce_fusion.1
  30.7 8.4 %fusion.11 = f32[4,2,8,2048]{3,2,0,1:T(8,128)S(1)} fusion(bf16[2,2,2048,2048]{3,2,1,0:T(8,128)(2,1)} %param.40, bf16[4,2,8,2048]{3,2,1,0:T(8,128)(2,1)S(1)} %all-to-all-done), kind=kOutput, calls=%fused_computation.9 | convolution fusion | flops 536870912 | bytes 17563648 | tf_op jit(solution)/shard_map/nlcd,lfd->nlcf/dot_general | solution.py:143
  39.1 8.7 %fusion.20 = bf16[4,2,8,2048]{3,2,0,1:T(8,128)(2,1)S(1)} fusion(bf16[2,2,2048,2048]{3,2,1,0:T(8,128)(2,1)} %param.40, f32[4,2,8,2048]{3,2,0,1:T(8,128)S(1)} %fusion.11, bf16[4,2,8,2048]{3,2,1,0:T(8,128)(2,1)S(1)} %all-to-all-done), kind=kOutput, calls=%fused_computation.13 | convolution fusion | flops 537657344 | bytes 17825792 | tf_op jit(solution)/shard_map/nlcd,lfd->nlcf/dot_general | solution.py:144
  47.9 9.5 %fusion.8 = f32[4,2,8,2048]{3,2,0,1:T(8,128)} fusion(bf16[4,2,8,2048]{3,2,0,1:T(8,128)(2,1)S(1)} %fusion.20, bf16[2,2048,2048]{2,1,0:T(8,128)(2,1)} %param.41), kind=kOutput, calls=%fused_computation.8 | convolution fusion | flops 536870912 | bytes 17563648 | tf_op jit(solution)/shard_map/nlcf,lfd->nlcd/dot_general | solution.py:146
  57.7 10.7 %psum.7 = f32[16,288]{1,0:T(8,128)S(1)} all-reduce(f32[16,288]{1,0:T(8,128)S(1)} %fusion.40), channel_id=1, replica_groups=mesh['parts'=2,'expert'=4,'tensor'=4] {'tensor'}, use_global_device_ids=true, to_apply=%region_1.2 | all-reduce | flops 4608 | bytes 36864 | tf_op jit(solution)/shard_map/psum | solution.py:32
  68.8 1.5 %multiply_reduce_fusion = (f32[16,1024]{1,0:T(8,128)S(1)}, f32[16,16,1024]{2,1,0:T(8,128)}) fusion(f32[16,16]{1,0:T(8,128)S(1)} %get-tuple-element.11, f32[16,16]{1,0:T(8,128)S(1)} %get-tuple-element.10, f32[16,1024]{1,0:T(8,128)S(1)} %get-tuple-element.7, f32[16,16,1024]{2,1,0:T(8,128)S(1)} %copy-done.1, f32[16,1024]{1,0:T(8,128)S(1)} %exp.29, ...), kind=kLoop, calls=%fused_computation.23 | loop fusion | flops 1556480 | bytes 2361344 | tf_op jit(solution)/shard_map/reduce_sum | solution.py:45
  70.3 9.9 %reduce-scatter.2.cloned.1.call-done = f32[4,2,8,512]{3,2,0,1:T(8,128)} async-done(((f32[4,2,8,2048]{3,2,0,1:T(8,128)}), f32[4,2,8,512]{3,2,0,1:T(8,128)}) %reduce-scatter.2.cloned.1.call-update) | async-done | bytes 131088 | tf_op jit(solution)/shard_map/reduce_scatter | solution.py:149
  80.2 1.5 %copy.50 = f32[4,2,8,512]{3,2,1,0:T(8,128)} copy(f32[4,2,8,512]{3,2,0,1:T(8,128)} %reduce-scatter.2.cloned.1.call-done) | data formatting | bytes 262144 | tf_op jit(solution)/shard_map/reduce_scatter | solution.py:149
  81.7 4.6 %all-to-all-start.1 = ((f32[4,2,8,512]{3,2,1,0:T(8,128)}), f32[4,2,8,512]{3,2,1,0:T(8,128)S(1)}, u32[]{:S(2)}, u32[]{:S(2)}) async-start(f32[4,2,8,512]{3,2,1,0:T(8,128)} %copy.50), calls=%async_computation.2 | async-start | bytes 262144 | tf_op jit(solution)/shard_map/all_to_all | solution.py:150
  86.3 0.7 fusion.36
  87.0 5.4 %all-to-all-done.1 = f32[4,2,8,512]{3,2,1,0:T(8,128)S(1)} async-done(((f32[4,2,8,512]{3,2,1,0:T(8,128)}), f32[4,2,8,512]{3,2,1,0:T(8,128)S(1)}, u32[]{:S(2)}, u32[]{:S(2)}) %all-to-all-start.1) | async-done | bytes 131104 | tf_op jit(solution)/shard_map/all_to_all | solution.py:150
  92.4 0.8 fusion.25
  (27 shorter events, 1.5 us)
Async XLA Ops:
  7.2 50.3 %copy-start = (bf16[288,1024]{1,0:T(8,128)(2,1)S(1)}, bf16[288,1024]{1,0:T(8,128)(2,1)}, u32[]{:S(2)}) copy-start(bf16[288,1024]{1,0:T(8,128)(2,1)} %param.27) | copy-start | bytes 1769476
  16.0 14.7 %all-to-all-start = ((bf16[4,2,8,2048]{3,2,1,0:T(8,128)(2,1)}), bf16[4,2,8,2048]{3,2,1,0:T(8,128)(2,1)S(1)}, u32[]{:S(2)}, u32[]{:S(2)}) async-start(bf16[4,2,8,2048]{3,2,1,0:T(8,128)(2,1)} %bitcast.6), calls=%async_computation | async-start | bytes 524288 | tf_op jit(solution)/shard_map/all_to_all | solution.py:142
  21.3 58.9 %reduce-scatter.2.cloned.1.call-start = ((), (), s32[]{:S(2)}) async-start(), calls=%async_computation.3 | async-start | bytes 655360 | tf_op jit(solution)/shard_map/reduce_scatter | solution.py:149
  47.8 9.7 %copy-start.3 = (f32[1024]{0:T(1024)S(1)}, f32[1024]{0:T(1024)}, u32[]{:S(2)}) copy-start(f32[1024]{0:T(1024)} %param.26) | copy-start | bytes 12292
  47.8 20.6 %copy-start.5 = (f32[16,2]{0,1:T(2,128)S(1)}, f32[16,2]{0,1:T(2,128)}, u32[]{:S(2)}) copy-start(f32[16,2]{0,1:T(2,128)} %param.39) | copy-start | bytes 388
  47.8 20.7 %copy-start.6 = (bf16[256,1024]{1,0:T(8,128)(2,1)S(1)}, bf16[256,1024]{1,0:T(8,128)(2,1)}, u32[]{:S(2)}) copy-start(bf16[256,1024]{1,0:T(8,128)(2,1)} %param.28) | copy-start | bytes 1572868
  47.8 20.7 %copy-start.7 = (f32[1024]{0:T(1024)S(1)}, f32[1024]{0:T(1024)}, u32[]{:S(2)}) copy-start(f32[1024]{0:T(1024)} %param.29) | copy-start | bytes 12292
  47.9 20.9 %copy-start.1 = (f32[16,16,1024]{2,1,0:T(8,128)S(1)}, f32[16,16,1024]{2,1,0:T(8,128)}, u32[]{:S(2)}) copy-start(f32[16,16,1024]{2,1,0:T(8,128)} %param.24) | copy-start | bytes 3145732
  47.9 38.5 %copy-start.2 = (bf16[16,1024]{1,0:T(8,128)(2,1)S(1)}, bf16[16,1024]{1,0:T(8,128)(2,1)}, u32[]{:S(2)}) copy-start(bf16[16,1024]{1,0:T(8,128)(2,1)} %param.22) | copy-start | bytes 98308
  47.9 38.5 %copy-start.4 = (f32[1024]{0:T(1024)S(1)}, f32[1024]{0:T(1024)}, u32[]{:S(2)}) copy-start(f32[1024]{0:T(1024)} %param.31) | copy-start | bytes 12292
  81.7 10.7 %all-to-all-start.1 = ((f32[4,2,8,512]{3,2,1,0:T(8,128)}), f32[4,2,8,512]{3,2,1,0:T(8,128)S(1)}, u32[]{:S(2)}, u32[]{:S(2)}) async-start(f32[4,2,8,512]{3,2,1,0:T(8,128)} %copy.50), calls=%async_computation.2 | async-start | bytes 262144 | tf_op jit(solution)/shard_map/all_to_all | solution.py:150
Sparse Core Ops, SparseCore 0:
  57.6 22.5 reduce-scatter.1
where the time goes:
time: 101 us; the launch traced here: 100 us
  matrix products  33.4 us (33%)
  blocking collectives  17.1 us (17%)
  waiting for transfers between devices  16 us (16%)
  between operations  14.2 us (14%)
  starting transfers between devices  9.95 us (10%)
  other arithmetic  6.26 us (6%)
  local copies, waits for them, and re-layouts  3.17 us (3%)
    psum x1, blocking collectives, mamba_step(): mixing = lax.psum(local_mix, 'tensor')  10.7 us
    reduce_scatter x1, waiting for transfers between devices, shards(): lax.psum_scatter(partial_value, 'tensor', scatter_dimension=3, tiled=True)  9.91 us
    dot_general x1, matrix products, shards(): jnp.einsum('nlcf,lfd->nlcd', hidden, outer_weights, preferred_element_typ...  9.55 us
    dot_general x1, matrix products, shards(): jnp.einsum('nlcd,lfd->nlcf', received, up_rows, preferred_element_type=jn...  8.68 us
    dot_general x1, matrix products, shards(): jnp.einsum('nlcd,lfd->nlcf', received, gate_rows, preferred_element_type=...  8.42 us
    all_gather x1, blocking collectives, shards(): features = lax.all_gather(expert_input, 'tensor', axis=1, tiled=True)  6.44 us
    all_to_all x1, waiting for transfers between devices, shards(): lax.all_to_all(share_sum, 'expert', split_axis=0, concat_axis=0, tiled=True)  5.4 us
    all_to_all x1, starting transfers between devices, shards(): lax.all_to_all(outgoing, 'expert', split_axis=0, concat_axis=0, tiled=True)  5.34 us
  transfers between devices with their start and end apart: 3, of which 3 were waited for; matrix products, arithmetic and copies ran while one was open for 11% of the time, Pallas kernels for 0%

commit v1 on v0

v1 whole, which is shorter than its diff:
```python
import functools

import jax
import jax.numpy as jnp
from jax import lax
from jax.experimental import pallas as pl
from jax.experimental.pallas import tpu as pltpu
from jax.sharding import PartitionSpec as P

EXPERTS = 8
MESH = pl.DeviceIdType.MESH
F32 = jnp.float32
BF16 = jnp.bfloat16
EXACT = lax.Precision.HIGHEST
NT = (((1,), (1,)), ((), ()))
NN = (((1,), (0,)), ((), ()))


def dot(a, b, dims):
    return lax.dot_general(a, b, dims, preferred_element_type=F32)


def eye(n):
    rows = lax.broadcasted_iota(jnp.int32, (n, n), 0)
    cols = lax.broadcasted_iota(jnp.int32, (n, n), 1)
    return jnp.where(rows == cols, 1.0, 0.0).astype(F32)


def kernel(
    E,
    T,
    fc,
    mi_h, mg_h, cs_h, ss_h, cw_h, cb_h, sp_h, tp_h, sb_h, dl_h, sg_h,
    q_h, ne_h, pe_h, len_h, xi_h, ro_h, ga_h, iw_h, ow_h,
    mo_h, ns_h, ao_h, eo_h,
    mi, mg, cs, ss, cw, cb, sp, tp, sb, dl, sg, q, ne, pe, lens, ro, ga, iw, ow,
    X, wr, mixp, mixr, conv, yv, stv, scuv, score, knew, vnew, ao, mo, hid, psend, rrecv, tot, tsend, erecv, eo,
    in_sem, pe_sem, iw_sem, ow_sem, out_sem, x_sem,
    as_sem, ar_sem, ws_sem, wr_sem, bs_sem, br_sem, ms_sem, mr_sem, rs_sem, rr_sem, es_sem, er_sem,
):
    me = lax.axis_index("expert")
    mt = lax.axis_index("tensor")
    B, Dl = xi_h.shape
    L, _, F, D = iw_h.shape
    S, H, HD = q_h.shape
    G = ne_h.shape[1]
    per = H // G
    N = dl_h.shape[0]
    R = tp_h.shape[0]
    reps = max(1, E // EXPERTS)
    nf = F // fc
    remote = functools.partial(pltpu.make_async_remote_copy, device_id_type=MESH)

    def epeer(d):
        return lax.rem(me + d, E)

    def tpeer(d):
        return lax.rem(mt + d, T)

    barrier = pltpu.get_barrier_semaphore()
    for d in range(1, E):
        pl.semaphore_signal(barrier, inc=1, device_id={"expert": epeer(d)}, device_id_type=MESH)
    for d in range(1, T):
        pl.semaphore_signal(barrier, inc=1, device_id={"tensor": tpeer(d)}, device_id_type=MESH)

    pairs = [
        (ro_h, ro), (ga_h, ga), (len_h, lens), (cs_h, cs), (mi_h, mi), (cw_h, cw), (cb_h, cb), (sp_h, sp),
        (q_h, q), (ne_h, ne), (tp_h, tp), (sb_h, sb), (dl_h, dl), (sg_h, sg), (mg_h, mg), (ss_h, ss),
    ]
    local = {}
    for n, (src, dst) in enumerate(pairs):
        local[id(dst)] = pltpu.make_async_copy(src, dst, in_sem.at[n])

    def block(e, t):
        return X.at[pl.ds(pl.multiple_of(e * B, B), B), pl.ds(pl.multiple_of(t * Dl, Dl), Dl)]

    def rows(ref, e):
        return ref.at[pl.ds(pl.multiple_of(e * B, B), B)]

    own_x = pltpu.make_async_copy(xi_h, block(me, mt), x_sem)
    early = [ro, ga, lens, cs, mi, cw, cb, sp, q, ne]
    late = [tp, sb, dl, sg, mg, ss]
    for dst in early:
        local[id(dst)].start()
    own_x.start()
    pcopy = pltpu.make_async_copy(pe_h, pe, pe_sem)
    pcopy.start()
    for dst in late:
        local[id(dst)].start()

    def inner_copy(l, i):
        at = pl.ds(pl.multiple_of(i * fc, fc), fc)
        return pltpu.make_async_copy(iw_h.at[l, :, at, :], iw.at[l, :, at, :], iw_sem.at[l, i])

    for l in range(L):
        @pl.loop(0, nf)
        def _(i, l=l):
            inner_copy(l, i).start()

    def outer_copy(j, l):
        cols = pl.ds(pl.multiple_of(tpeer(j + 1) * Dl, Dl), Dl)
        return pltpu.make_async_copy(ow_h.at[l, :, cols], ow.at[j, pl.ds(l * F, F), :], ow_sem.at[j, l])

    for j in range(T):
        for l in range(L):
            outer_copy(j, l).start()

    local[id(ro)].wait()
    local[id(ga)].wait()
    width = wr.shape[1]
    table = jnp.zeros((width, B), F32)
    row_of = lax.broadcasted_iota(jnp.int32, (width, B), 0)
    for k in range(ro.shape[0]):
        first = ro[k : k + 1, :] * reps
        table = table + jnp.where((row_of >= first) & (row_of < first + reps), ga[k : k + 1, :], 0.0)
    table = lax.dot_general(eye(B), table, NT, precision=EXACT, preferred_element_type=F32)
    wr[pl.ds(pl.multiple_of(me * B, B), B), :] = table

    pl.semaphore_wait(barrier, E - 1 + T - 1)

    def send_a(d):
        p = epeer(d)
        return remote(src_ref=xi_h, dst_ref=block(me, mt), send_sem=as_sem.at[p], recv_sem=ar_sem.at[me],
                      device_id={"expert": p})

    def recv_a(e):
        return remote(src_ref=xi_h, dst_ref=block(e, mt), send_sem=as_sem.at[e], recv_sem=ar_sem.at[e],
                      device_id={"expert": e})

    def send_w(d):
        p = epeer(d)
        return remote(src_ref=rows(wr, me), dst_ref=rows(wr, me), send_sem=ws_sem.at[p], recv_sem=wr_sem.at[me],
                      device_id={"expert": p})

    def recv_w(e):
        return remote(src_ref=rows(wr, e), dst_ref=rows(wr, e), send_sem=ws_sem.at[e], recv_sem=wr_sem.at[e],
                      device_id={"expert": e})

    def send_b(e, d, own):
        p = tpeer(d)
        return remote(src_ref=xi_h if own else block(e, mt), dst_ref=block(e, mt), send_sem=bs_sem.at[e, p],
                      recv_sem=br_sem.at[e, mt], device_id={"tensor": p})

    def recv_b(e, t):
        return remote(src_ref=xi_h, dst_ref=block(e, t), send_sem=bs_sem.at[e, t], recv_sem=br_sem.at[e, t],
                      device_id={"tensor": t})

    for d in range(1, E):
        send_a(d).start()
    for d in range(1, T):
        send_b(me, d, True).start()
    for d in range(1, E):
        send_w(d).start()

    for ref in (cs, mi, cw, cb, sp):
        local[id(ref)].wait()
    taps = cw.shape[0]
    pre = mi[...].astype(F32) * cw[taps - 1 : taps, :]
    for k in range(taps - 1):
        pre = pre + cs[k].astype(F32) * cw[k : k + 1, :]
    act = jax.nn.silu(pre + cb[...])
    conv[...] = act
    mixp[...] = dot(act.astype(BF16), sp[...], NT)

    def send_m(d):
        p = tpeer(d)
        return remote(src_ref=mixp, dst_ref=mixr.at[mt], send_sem=ms_sem.at[p], recv_sem=mr_sem.at[mt],
                      device_id={"tensor": p})

    def recv_m(t):
        return remote(src_ref=mixp, dst_ref=mixr.at[t], send_sem=ms_sem.at[t], recv_sem=mr_sem.at[t],
                      device_id={"tensor": t})

    for d in range(1, T):
        send_m(d).start()

    for ref in (lens, q, ne):
        local[id(ref)].wait()
    pcopy.wait()
    head_row = lax.broadcasted_iota(jnp.int32, (H, HD), 0)
    places = lax.broadcasted_iota(jnp.int32, (H, pe.shape[2]), 1)
    place_row = lax.broadcasted_iota(jnp.int32, (H, pe.shape[2]), 0)

    def by_group(parts, row):
        out = parts[0]
        for g in range(1, G):
            out = jnp.where(row >= g * per, parts[g], out)
        return out

    for s in range(S):
        qs = q[s]
        sc = by_group([dot(qs, pe[s, g, :, :HD], NT) for g in range(G)], place_row)
        score[s] = jnp.where(places < lens[s], sc, -jnp.inf)
        entry = ne[s].astype(F32)
        knew[s] = by_group([jnp.broadcast_to(entry[g : g + 1, :HD], (H, HD)) for g in range(G)], head_row)
        vnew[s] = by_group([jnp.broadcast_to(entry[g : g + 1, HD:], (H, HD)) for g in range(G)], head_row)

    for d in range(1, E):
        e = epeer(d)
        recv_a(e).wait_recv()
        for k in range(1, T):
            send_b(e, k, False).start()

    scaling = HD ** (-0.5)
    sc = score[...] * scaling
    own_score = jnp.sum(q[...].astype(F32) * knew[...], axis=2, keepdims=True) * scaling
    highest = jnp.maximum(jnp.max(sc, axis=2, keepdims=True), own_score)
    weights = jnp.exp(sc - highest)
    own_weight = jnp.exp(own_score - highest)
    total = jnp.sum(weights, axis=2, keepdims=True) + own_weight
    score[...] = weights / total
    vnew[...] = (own_weight / total).astype(BF16).astype(F32) * vnew[...]
    for s in range(S):
        low = score[s].astype(BF16)
        mixed = by_group([dot(low, pe[s, g, :, HD:], NN) for g in range(G)], head_row)
        knew[s] = mixed + vnew[s]
    for h in range(H):
        ao[:, h * HD : (h + 1) * HD] = knew[:, h, :].astype(BF16)
    out_a = pltpu.make_async_copy(ao, ao_h, out_sem.at[0])
    out_a.start()

    for ref in (tp, sb, dl, sg, mg, ss):
        local[id(ref)].wait()
    mixing = mixp[...]
    for d in range(1, T):
        t = tpeer(d)
        recv_m(t).wait_recv()
        mixing = mixing + mixr[t]
    step = jax.nn.softplus(dot(mixing[:, :R].astype(BF16), tp[...], NN) + sb[...])
    stv[...] = step
    scuv[...] = step * conv[...]
    coef = lax.dot_general(mixing[:, R:], eye(S), (((0,), (0,)), ((), ())), precision=EXACT, preferred_element_type=F32)
    decay = jnp.exp(dl[...])
    for s in range(S):
        nxt = jnp.exp(-stv[s : s + 1, :] * decay) * ss[s] + scuv[s : s + 1, :] * coef[:N, s : s + 1]
        ss[s] = nxt
        yv[s : s + 1, :] = jnp.sum(nxt * coef[N:, s : s + 1], axis=0, keepdims=True)
    out_s = pltpu.make_async_copy(ss, ns_h, out_sem.at[1])
    out_s.start()
    mo[...] = ((yv[...] + sg[...] * conv[...]) * jax.nn.silu(mg[...].astype(F32))).astype(BF16)
    out_m = pltpu.make_async_copy(mo, mo_h, out_sem.at[2])
    out_m.start()

    own_x.wait()
    for d in range(1, E):
        recv_w(epeer(d)).wait_recv()
    for e in range(E):
        for d in range(1, T):
            recv_b(lax.rem(me + e, E), tpeer(d)).wait_recv()
    lanes = lax.broadcasted_iota(jnp.int32, wr.shape, 1)
    for l in range(L):
        weight = jnp.sum(jnp.where(lanes == me * L + l, wr[...], 0.0), axis=1, keepdims=True)

        @pl.loop(0, nf)
        def _(i, l=l, weight=weight):
            inner_copy(l, i).wait()
            at = pl.ds(pl.multiple_of(i * fc, fc), fc)
            x = X[...]
            gate = dot(x, iw[l, 0, at, :], NT)
            up = dot(x, iw[l, 1, at, :], NT)
            to = pl.ds(pl.multiple_of(l * F + i * fc, fc), fc)
            hid[:, to] = (jax.nn.silu(gate) * up * weight).astype(BF16)

    def send_r(j):
        p = tpeer(j + 1)
        return remote(src_ref=psend.at[j], dst_ref=rrecv.at[mt], send_sem=rs_sem.at[j], recv_sem=rr_sem.at[mt],
                      device_id={"tensor": p})

    def recv_r(t):
        return remote(src_ref=psend.at[0], dst_ref=rrecv.at[t], send_sem=rs_sem.at[0], recv_sem=rr_sem.at[t],
                      device_id={"tensor": t})

    for j in range(T):
        for l in range(L):
            outer_copy(j, l).wait()
        part = dot(hid[...], ow[j], NN)
        if j < T - 1:
            psend[j] = part.astype(BF16)
            send_r(j).start()
    for d in range(1, T):
        t = tpeer(d)
        recv_r(t).wait_recv()
        part = part + rrecv[t].astype(F32)
    tot[...] = part
    tsend[...] = part.astype(BF16)

    def send_e(d):
        p = epeer(d)
        return remote(src_ref=rows(tsend, p), dst_ref=erecv.at[me], send_sem=es_sem.at[p], recv_sem=er_sem.at[me],
                      device_id={"expert": p})

    def recv_e(e):
        return remote(src_ref=rows(tsend, e), dst_ref=erecv.at[e], send_sem=es_sem.at[e], recv_sem=er_sem.at[e],
                      device_id={"expert": e})

    for d in range(1, E):
        send_e(d).start()
    final = tot[pl.ds(pl.multiple_of(me * B, B), B), :]
    for d in range(1, E):
        e = epeer(d)
        recv_e(e).wait_recv()
        final = final + erecv[e].astype(F32)
    eo[...] = final.astype(BF16)
    out_e = pltpu.make_async_copy(eo, eo_h, out_sem.at[3])
    out_e.start()

    for d in range(1, E):
        send_a(d).wait_send()
        send_w(d).wait_send()
        send_e(d).wait_send()
    for d in range(1, T):
        send_b(me, d, True).wait_send()
        send_m(d).wait_send()
        for k in range(1, E):
            send_b(epeer(k), d, False).wait_send()
    for j in range(T - 1):
        send_r(j).wait_send()
    for copy in (out_a, out_s, out_m, out_e):
        copy.wait()


def shards(
    mamba_input,
    mamba_gate,
    conv_state,
    scan_state,
    conv_weight,
    conv_bias,
    state_proj,
    step_proj,
    step_bias,
    decay_log,
    skip_gain,
    queries,
    new_entry,
    past_entries,
    lengths,
    expert_input,
    routes,
    slots,
    gates,
    inner_weights,
    outer_weights,
):
    E = lax.axis_size("expert")
    T = lax.axis_size("tensor")
    B, Dl = expert_input.shape
    L, _, F, D = inner_weights.shape
    S, H, HD = queries.shape
    C = mamba_input.shape[1]
    M = state_proj.shape[0]
    fc = min(F, 256)
    total_rows = E * L
    width = -(-total_rows // 128) * 128
    args = [
        mamba_input,
        mamba_gate,
        conv_state.transpose(1, 0, 2),
        scan_state,
        conv_weight,
        conv_bias.reshape(1, C),
        state_proj,
        step_proj,
        step_bias.reshape(1, C),
        decay_log,
        skip_gain.reshape(1, C),
        queries,
        new_entry,
        past_entries,
        lengths,
        expert_input,
        routes.T,
        gates.T,
        inner_weights,
        outer_weights,
    ]

    def held(a):
        return pltpu.VMEM(a.shape, a.dtype)

    outs = (
        jax.ShapeDtypeStruct((B, C), BF16),
        jax.ShapeDtypeStruct(scan_state.shape, F32),
        jax.ShapeDtypeStruct((S, H * HD), BF16),
        jax.ShapeDtypeStruct((B, Dl), BF16),
    )
    scratch = [held(a) for a in args[:14]] + [pltpu.SMEM(lengths.shape, jnp.int32), held(args[16]), held(args[17])]
    scratch += [held(inner_weights), pltpu.VMEM((T, L * F, Dl), BF16)]
    scratch += [
        pltpu.VMEM((E * B, D), BF16),
        pltpu.VMEM((E * B, width), F32),
        pltpu.VMEM((B, M), F32),
        pltpu.VMEM((T, B, M), F32),
        pltpu.VMEM((B, C), F32),
        pltpu.VMEM((B, C), F32),
        pltpu.VMEM((B, C), F32),
        pltpu.VMEM((B, C), F32),
        pltpu.VMEM((S, H, past_entries.shape[2]), F32),
        pltpu.VMEM((S, H, HD), F32),
        pltpu.VMEM((S, H, HD), F32),
        pltpu.VMEM((S, H * HD), BF16),
        pltpu.VMEM((B, C), BF16),
        pltpu.VMEM((E * B, L * F), BF16),
        pltpu.VMEM((T - 1, E * B, Dl), BF16),
        pltpu.VMEM((T, E * B, Dl), BF16),
        pltpu.VMEM((E * B, Dl), F32),
        pltpu.VMEM((E * B, Dl), BF16),
        pltpu.VMEM((E, B, Dl), BF16),
        pltpu.VMEM((B, Dl), BF16),
    ]
    sem = pltpu.SemaphoreType.DMA
    scratch += [sem((16,)), sem, sem((L, F // fc)), sem((T, L)), sem((4,)), sem]
    scratch += [sem((E,)), sem((E,)), sem((E,)), sem((E,)), sem((E, T)), sem((E, T)), sem((T,)), sem((T,))]
    scratch += [sem((T,)), sem((T,)), sem((E,)), sem((E,))]
    anywhere = pl.BlockSpec(memory_space=pl.ANY)
    mamba_out, next_state, attention_out, expert_out = pl.pallas_call(
        functools.partial(kernel, E, T, fc),
        out_shape=outs,
        in_specs=[anywhere] * len(args),
        out_specs=[anywhere] * len(outs),
        scratch_shapes=scratch,
        compiler_params=pltpu.CompilerParams(
            collective_id=0, has_side_effects=True, vmem_limit_bytes=67043328
        ),
    )(*args)
    return (mamba_out, next_state, attention_out, expert_out)


def solution(mesh):
    return jax.shard_map(
        shards,
        mesh=mesh,
        in_specs=(
            P(("parts", "expert"), "tensor"),
            P(("parts", "expert"), "tensor"),
            P(("parts", "expert"), None, "tensor"),
            P(("parts", "expert"), None, "tensor"),
            P(None, "tensor"),
            P("tensor"),
            P(None, "tensor"),
            P(None, "tensor"),
            P("tensor"),
            P(None, "tensor"),
            P("tensor"),
            P(("parts", "expert"), "tensor", None),
            P(("parts", "expert"), "tensor", None),
            P(("parts", "expert"), "tensor", None, None),
            P(("parts", "expert")),
            P(("parts", "expert"), "tensor"),
            P(("parts", "expert"), None),
            P(("parts", "expert"), None),
            P(("parts", "expert"), None),
            P("expert", None, "tensor", None),
            P("expert", "tensor", None),
        ),
        out_specs=(
            P(("parts", "expert"), "tensor"),
            P(("parts", "expert"), None, "tensor"),
            P(("parts", "expert"), "tensor"),
            P(("parts", "expert"), "tensor"),
        ),
        check_vma=False,
    )
```

time: 101 us -> 42.9 us (0.42)
  Pallas kernels: 0 us -> 35.5 us
  matrix products: 33.4 us -> 0 us
  blocking collectives: 17.1 us -> 0 us
  waiting for transfers between devices: 16 us -> 0 us
  between operations: 14.2 us -> 0.65 us
  starting transfers between devices: 9.95 us -> 0 us
  other arithmetic: 6.26 us -> 0 us
  local copies, waits for them, and re-layouts: 3.17 us -> 6.38 us
    pallas_call x0 -> x1, Pallas kernels: none -> 35.5 us  [shards(): pl.pallas_call(functools.partial(kernel, E, T, fc), out_shape=outs, in_sp...]
    dot_general x10 -> x0, matrix products: 33.4 us -> none  [the longest x1 9.55 us: shards(): jnp.einsum('nlcf,lfd->nlcd', hidden, outer_weights, preferred_element_typ...]
    psum x1 -> x0, blocking collectives: 10.7 us -> none  [mamba_step(): mixing = lax.psum(local_mix, 'tensor')]
    all_to_all x2 -> x0, starting transfers between devices: 9.94 us -> none  [the longest x1 5.34 us: shards(): lax.all_to_all(outgoing, 'expert', split_axis=0, concat_axis=0, tiled=True)]
    reduce_scatter x1 -> x0, waiting for transfers between devices: 9.91 us -> none  [shards(): lax.psum_scatter(partial_value, 'tensor', scatter_dimension=3, tiled=True)]
    all_gather x1 -> x0, blocking collectives: 6.44 us -> none  [shards(): features = lax.all_gather(expert_input, 'tensor', axis=1, tiled=True)]
    unnamed x16 -> x4, local copies, waits for them, and re-layouts: 0.05 us -> 6.38 us
    all_to_all x2 -> x0, waiting for transfers between devices: 6.02 us -> none  [the longest x1 5.4 us: shards(): lax.all_to_all(share_sum, 'expert', split_axis=0, concat_axis=0, tiled=True)]
  transfers between devices with their start and end apart: 3 -> 0, of which waited for: 3 -> 0; matrix products, arithmetic and copies ran while one was open for 11% -> 0% of each run, Pallas kernels for 0% -> 0%
where the time goes in v1:
time: 42.9 us; the launch traced here: 42.6 us
  Pallas kernels  35.5 us (83%)
  local copies, waits for them, and re-layouts  6.38 us (15%)
  between operations  0.65 us (2%)
    pallas_call x1, Pallas kernels, shards(): pl.pallas_call(functools.partial(kernel, E, T, fc), out_shape=outs, in_sp...  35.5 us
    unnamed x4, local copies, waits for them, and re-layouts  6.38 us

profile of v1, /device:TPU:0, one launch (start us, length us, event | category | flops | bytes accessed | tf_op | source)
XLA Modules:
  0.0 42.6 jit_solution(2357224422272604045)
XLA Ops:
  0.6 35.5 %shard_map.219 = (bf16[16,1024]{1,0:T(8,128)(2,1)}, f32[16,16,1024]{2,1,0:T(8,128)}, bf16[16,1024]{1,0:T(8,128)(2,1)}, bf16[16,512]{1,0:T(8,128)(2,1)}) custom-call(bf16[16,1024]{1,0:T(8,128)(2,1)} %mi_h.1, bf16[16,1024]{1,0:T(8,128)(2,1)} %mg_h.1, bf16[3,16,1024]{2,1,0:T(8,128)(2,1)} %bitcast.6, f32[16,16,1024]{2,1,0:T(8,128)} %ss_h.1, f32[4,1024]{1,0:T(4,128)} %cw_h.1, ...), custom_call_target="tpu_custom_call" | custom-call | tf_op jit(solution)/shard_map/pallas_call | solution.py:416
  36.2 1.4 %copy.28 = bf16[16,1024]{1,0:T(8,128)(2,1)} copy(bf16[16,1024]{1,0:T(8,128)(2,1)} %get-tuple-element.8) | data formatting | bytes 65536
  37.6 2.3 %copy.29 = f32[16,16,1024]{2,1,0:T(8,128)} copy(f32[16,16,1024]{2,1,0:T(8,128)} %get-tuple-element.9) | data formatting | bytes 2097152
  39.9 1.4 %copy.30 = bf16[16,1024]{1,0:T(8,128)(2,1)} copy(bf16[16,1024]{1,0:T(8,128)(2,1)} %get-tuple-element.10) | data formatting | bytes 65536
  41.2 1.3 %copy.31 = bf16[16,512]{1,0:T(8,128)(2,1)} copy(bf16[16,512]{1,0:T(8,128)(2,1)} %get-tuple-element.11) | data formatting | bytes 32768

commit v2 on v1

--- a/solution.py
+++ b/solution.py
@@ -55,7 +55,17 @@
         return lax.rem(me + d, E)
 
     def tpeer(d):
-        return lax.rem(mt + d, T)
+        d = d % T
+        if T & (T - 1):
+            return lax.rem(mt + d, T)
+        d = T - d if d else 0
+        p = mt
+        bit = 1
+        while bit < T:
+            if d & bit:
+                p = p + bit - 2 * bit * lax.rem(p // bit, 2)
+            bit *= 2
+        return p
 
     barrier = pltpu.get_barrier_semaphore()
     for d in range(1, E):
@@ -174,9 +184,6 @@
     for d in range(1, T):
         send_m(d).start()
 
-    for ref in (lens, q, ne):
-        local[id(ref)].wait()
-    pcopy.wait()
     head_row = lax.broadcasted_iota(jnp.int32, (H, HD), 0)
     places = lax.broadcasted_iota(jnp.int32, (H, pe.shape[2]), 1)
     place_row = lax.broadcasted_iota(jnp.int32, (H, pe.shape[2]), 0)
@@ -187,60 +194,72 @@
             out = jnp.where(row >= g * per, parts[g], out)
         return out
 
-    for s in range(S):
-        qs = q[s]
-        sc = by_group([dot(qs, pe[s, g, :, :HD], NT) for g in range(G)], place_row)
-        score[s] = jnp.where(places < lens[s], sc, -jnp.inf)
-        entry = ne[s].astype(F32)
-        knew[s] = by_group([jnp.broadcast_to(entry[g : g + 1, :HD], (H, HD)) for g in range(G)], head_row)
-        vnew[s] = by_group([jnp.broadcast_to(entry[g : g + 1, HD:], (H, HD)) for g in range(G)], head_row)
-
-    for d in range(1, E):
-        e = epeer(d)
-        recv_a(e).wait_recv()
-        for k in range(1, T):
-            send_b(e, k, False).start()
-
-    scaling = HD ** (-0.5)
-    sc = score[...] * scaling
-    own_score = jnp.sum(q[...].astype(F32) * knew[...], axis=2, keepdims=True) * scaling
-    highest = jnp.maximum(jnp.max(sc, axis=2, keepdims=True), own_score)
-    weights = jnp.exp(sc - highest)
-    own_weight = jnp.exp(own_score - highest)
-    total = jnp.sum(weights, axis=2, keepdims=True) + own_weight
-    score[...] = weights / total
-    vnew[...] = (own_weight / total).astype(BF16).astype(F32) * vnew[...]
-    for s in range(S):
-        low = score[s].astype(BF16)
-        mixed = by_group([dot(low, pe[s, g, :, HD:], NN) for g in range(G)], head_row)
-        knew[s] = mixed + vnew[s]
-    for h in range(H):
-        ao[:, h * HD : (h + 1) * HD] = knew[:, h, :].astype(BF16)
-    out_a = pltpu.make_async_copy(ao, ao_h, out_sem.at[0])
-    out_a.start()
-
-    for ref in (tp, sb, dl, sg, mg, ss):
-        local[id(ref)].wait()
-    mixing = mixp[...]
-    for d in range(1, T):
-        t = tpeer(d)
-        recv_m(t).wait_recv()
-        mixing = mixing + mixr[t]
-    step = jax.nn.softplus(dot(mixing[:, :R].astype(BF16), tp[...], NN) + sb[...])
-    stv[...] = step
-    scuv[...] = step * conv[...]
-    coef = lax.dot_general(mixing[:, R:], eye(S), (((0,), (0,)), ((), ())), precision=EXACT, preferred_element_type=F32)
-    decay = jnp.exp(dl[...])
-    for s in range(S):
-        nxt = jnp.exp(-stv[s : s + 1, :] * decay) * ss[s] + scuv[s : s + 1, :] * coef[:N, s : s + 1]
-        ss[s] = nxt
-        yv[s : s + 1, :] = jnp.sum(nxt * coef[N:, s : s + 1], axis=0, keepdims=True)
-    out_s = pltpu.make_async_copy(ss, ns_h, out_sem.at[1])
-    out_s.start()
-    mo[...] = ((yv[...] + sg[...] * conv[...]) * jax.nn.silu(mg[...].astype(F32))).astype(BF16)
-    out_m = pltpu.make_async_copy(mo, mo_h, out_sem.at[2])
-    out_m.start()
-
+    def attention_scores():
+        for ref in (lens, q, ne):
+            local[id(ref)].wait()
+        pcopy.wait()
+        for s in range(S):
+            qs = q[s]
+            sc = by_group([dot(qs, pe[s, g, :, :HD], NT) for g in range(G)], place_row)
+            score[s] = jnp.where(places < lens[s], sc, -jnp.inf)
+            entry = ne[s].astype(F32)
+            knew[s] = by_group([jnp.broadcast_to(entry[g : g + 1, :HD], (H, HD)) for g in range(G)], head_row)
+            vnew[s] = by_group([jnp.broadcast_to(entry[g : g + 1, HD:], (H, HD)) for g in range(G)], head_row)
+
+    def forward():
+        for d in range(1, E):
+            e = epeer(d)
+            recv_a(e).wait_recv()
+            for k in range(1, T):
+                send_b(e, k, False).start()
+
+    def attention_rest():
+        scaling = HD ** (-0.5)
+        sc = score[...] * scaling
+        own_score = jnp.sum(q[...].astype(F32) * knew[...], axis=2, keepdims=True) * scaling
+        highest = jnp.maximum(jnp.max(sc, axis=2, keepdims=True), own_score)
+        weights = jnp.exp(sc - highest)
+        own_weight = jnp.exp(own_score - highest)
+        total = jnp.sum(weights, axis=2, keepdims=True) + own_weight
+        score[...] = weights / total
+        vnew[...] = (own_weight / total).astype(BF16).astype(F32) * vnew[...]
+        for s in range(S):
+            low = score[s].astype(BF16)
+            mixed = by_group([dot(low, pe[s, g, :, HD:], NN) for g in range(G)], head_row)
+            knew[s] = mixed + vnew[s]
+        for h in range(H):
+            ao[:, h * HD : (h + 1) * HD] = knew[:, h, :].astype(BF16)
+        out_a = pltpu.make_async_copy(ao, ao_h, out_sem.at[0])
+        out_a.start()
+        return out_a
+
+    def mamba():
+        for ref in (tp, sb, dl, sg, mg, ss):
+            local[id(ref)].wait()
+        mixing = mixp[...]
+        for d in range(1, T):
+            t = tpeer(d)
+            recv_m(t).wait_recv()
+            mixing = mixing + mixr[t]
+        step = jax.nn.softplus(dot(mixing[:, :R].astype(BF16), tp[...], NN) + sb[...])
+        stv[...] = step
+        scuv[...] = step * conv[...]
+        coef = lax.dot_general(mixing[:, R:], eye(S), (((0,), (0,)), ((), ())), precision=EXACT, preferred_element_type=F32)
+        decay = jnp.exp(dl[...])
+        for s in range(S):
+            nxt = jnp.exp(-stv[s : s + 1, :] * decay) * ss[s] + scuv[s : s + 1, :] * coef[:N, s : s + 1]
+            ss[s] = nxt
+            yv[s : s + 1, :] = jnp.sum(nxt * coef[N:, s : s + 1], axis=0, keepdims=True)
+        out_s = pltpu.make_async_copy(ss, ns_h, out_sem.at[1])
+        out_s.start()
+        mo[...] = ((yv[...] + sg[...] * conv[...]) * jax.nn.silu(mg[...].astype(F32))).astype(BF16)
+        out_m = pltpu.make_async_copy(mo, mo_h, out_sem.at[2])
+        out_m.start()
+        return (out_s, out_m)
+
+    forward()
+    attention_scores()
+    out_a = attention_rest()
     own_x.wait()
     for d in range(1, E):
         recv_w(epeer(d)).wait_recv()
@@ -295,6 +314,7 @@
 
     for d in range(1, E):
         send_e(d).start()
+    out_s, out_m = mamba()
     final = tot[pl.ds(pl.multiple_of(me * B, B), B), :]
     for d in range(1, E):
         e = epeer(d)
@@ -317,6 +337,30 @@
         send_r(j).wait_send()
     for copy in (out_a, out_s, out_m, out_e):
         copy.wait()
+
+
+def hand_over(*refs):
+    count = (len(refs) - 2) // 3
+    sources, results, held = refs[:count], refs[count : 2 * count], refs[2 * count : 3 * count]
+    in_sem, out_sem = refs[3 * count :]
+    steps = []
+    for n in range(count):
+        pieces = 4 if len(sources[n].shape) == 3 else 1
+        size = sources[n].shape[0] // pieces
+        for k in range(pieces):
+            at = pl.ds(k * size, size)
+            slot = len(steps)
+            steps.append((
+                pltpu.make_async_copy(sources[n].at[at], held[n].at[at], in_sem.at[slot]),
+                pltpu.make_async_copy(held[n].at[at], results[n].at[at], out_sem.at[slot]),
+            ))
+    for fetch, _ in steps:
+        fetch.start()
+    for fetch, put in steps:
+        fetch.wait()
+        put.start()
+    for _, put in steps:
+        put.wait()
 
 
 def shards(
@@ -349,7 +393,7 @@
     S, H, HD = queries.shape
     C = mamba_input.shape[1]
     M = state_proj.shape[0]
-    fc = min(F, 256)
+    fc = min(F, 1024)
     total_rows = E * L
     width = -(-total_rows // 128) * 128
     args = [
@@ -423,6 +467,14 @@
             collective_id=0, has_side_effects=True, vmem_limit_bytes=67043328
         ),
     )(*args)
+    results = (next_state, mamba_out, attention_out, expert_out)
+    next_state, mamba_out, attention_out, expert_out = pl.pallas_call(
+        hand_over,
+        out_shape=tuple(jax.ShapeDtypeStruct(a.shape, a.dtype) for a in results),
+        in_specs=[anywhere] * len(results),
+        out_specs=[anywhere] * len(results),
+        scratch_shapes=[held(a) for a in results] + [sem((8,)), sem((8,))],
+    )(*results)
     return (mamba_out, next_state, attention_out, expert_out)
 
 

time: 42.9 us -> 37.2 us (0.87)
  local copies, waits for them, and re-layouts: 6.38 us -> 0 us
  Pallas kernels: 35.5 us -> 36.4 us
    unnamed x4 -> x0, local copies, waits for them, and re-layouts: 6.38 us -> none
    pallas_call x0 -> x1, Pallas kernels: none -> 2.06 us  [shards(): pl.pallas_call(hand_over, out_shape=tuple((jax.ShapeDtypeStruct(a.shape,...]
    pallas_call x1, Pallas kernels: 35.5 us -> 34.3 us  [shards(): pl.pallas_call(functools.partial(kernel, E, T, fc), out_shape=outs, in_sp...]
where the time goes in v2:
time: 37.2 us; the launch traced here: 37 us
  Pallas kernels  36.4 us (98%)
  between operations  0.65 us (2%)
    pallas_call x1, Pallas kernels, shards(): pl.pallas_call(functools.partial(kernel, E, T, fc), out_shape=outs, in_sp...  34.3 us
    pallas_call x1, Pallas kernels, shards(): pl.pallas_call(hand_over, out_shape=tuple((jax.ShapeDtypeStruct(a.shape,...  2.06 us

profile of v2, /device:TPU:0, one launch (start us, length us, event | category | flops | bytes accessed | tf_op | source)
XLA Modules:
  0.0 37.0 jit_solution(1899243776702268391)
XLA Ops:
  0.6 34.3 %shard_map.219 = (bf16[16,1024]{1,0:T(8,128)(2,1)}, f32[16,16,1024]{2,1,0:T(8,128)}, bf16[16,1024]{1,0:T(8,128)(2,1)}, bf16[16,512]{1,0:T(8,128)(2,1)}) custom-call(bf16[16,1024]{1,0:T(8,128)(2,1)} %mi_h.1, bf16[16,1024]{1,0:T(8,128)(2,1)} %mg_h.1, bf16[3,16,1024]{2,1,0:T(8,128)(2,1)} %bitcast.6, f32[16,16,1024]{2,1,0:T(8,128)} %ss_h.1, f32[4,1024]{1,0:T(4,128)} %cw_h.1, ...), custom_call_target="tpu_custom_call" | custom-call | tf_op jit(solution)/shard_map/pallas_call | solution.py:460
  35.0 2.1 %shard_map.220 = (f32[16,16,1024]{2,1,0:T(8,128)}, bf16[16,1024]{1,0:T(8,128)(2,1)}, bf16[16,1024]{1,0:T(8,128)(2,1)}, bf16[16,512]{1,0:T(8,128)(2,1)}) custom-call(f32[16,16,1024]{2,1,0:T(8,128)} %get-tuple-element.12.refs_0_, bf16[16,1024]{1,0:T(8,128)(2,1)} %get-tuple-element.13.refs_1_, bf16[16,1024]{1,0:T(8,128)(2,1)} %get-tuple-element.14.refs_2_, ...), custom_call_target="tpu_custom_call" | custom-call | tf_op jit(solution)/shard_map/pallas_call | solution.py:471
